TPU v7x, 256 devices: a whole 4x4x8 slice. The times are simulated.
256 devices in a mesh: pair: 16 (over z, core), red: 16 (over x, y).
Axes of the slice: x: 4, y: 4, z: 8, core: 2. Of those that a mesh axis runs over, the one named last changes fastest.
Arguments:
- three_center: bfloat16 [2304, 256, 256], P('pair', 'red'), may hold values from -0.375 to 0.375
- occ_src: int32 [256, 16], P('red'), may hold values from 0 to 15, as said below
- occ_block: int32 [256, 16], P('red'), may hold values from 0 to 31
- occ_blocks: bfloat16 [512, 256], P('red'), may hold values from -0.375 to 0.375
- virt_block: int32 [16, 16, 1], P('red'), may hold values from 0 to 31, as said below
- virt_blocks: bfloat16 [16, 32, 256], P('red', 'pair'), may hold values from -1.5 to 1.5
Outputs:
- chi: float32 [2304, 2304], P('pair', 'red')
Inputs may be any that keep to these rules, and one draw needn't show every extreme that they name: `occ_src`: the 16 entries of a row are distinct. `virt_block`: every block listed for tile t of a red group lies from (t) * 2 to (t) * 2 + 1.
All inputs are finite; a program needn't handle non-finite values.
Results may differ from a plain program's by a relative error of at most 0.0041.
Values may be sent and summed in bfloat16 or wider, within the bound.
A program may use at most 128 MiB of HBM per device.

v0:
```python
import jax
import jax.numpy as jnp
from jax import lax
from jax.sharding import PartitionSpec as P

BLK = 16
TPD = 1


def occupied(three_center, occ_src, occ_block, occ_blocks):
    aux_rows, ntiles, area = three_center.shape
    nblocks = occ_blocks.shape[0]
    block_hot = (
        occ_block[:, :, None] == jnp.arange(nblocks, dtype=jnp.int32)[None, None, :]
    ).astype(jnp.bfloat16)
    picked = jnp.einsum(
        "tsb,bk->tsk", block_hot, occ_blocks, preferred_element_type=jnp.float32
    ).astype(jnp.bfloat16)
    source_hot = (occ_src[:, :, None] == jnp.arange(ntiles, dtype=jnp.int32)[None, None, :]).astype(
        jnp.bfloat16
    )
    mixing = jnp.einsum(
        "tsk,tsa->tka", source_hot, picked, preferred_element_type=jnp.float32
    ).astype(jnp.bfloat16)
    mixing = mixing.reshape(ntiles, ntiles, BLK, BLK)
    blocks = three_center.reshape(aux_rows, ntiles, BLK, BLK)
    half = jnp.einsum("tkml,pkln->ptmn", mixing, blocks, preferred_element_type=jnp.float32)
    return half.reshape(aux_rows, ntiles, area).astype(jnp.bfloat16)


def virtual(half, listed, blocks):
    aux_rows, ntiles, area = half.shape
    owners = listed.shape[0]
    nblocks = blocks.shape[0]
    block_hot = (listed[..., None] == jnp.arange(nblocks, dtype=jnp.int32)).astype(jnp.bfloat16)
    picked = jnp.einsum(
        "oijb,bk->oijk", block_hot, blocks, preferred_element_type=jnp.float32
    ).astype(jnp.bfloat16)
    picked = picked.reshape(owners, TPD, TPD, BLK, BLK)
    grouped = half.reshape(aux_rows, owners, TPD, BLK, BLK)
    kernel = jnp.einsum("pojml,oijln->poimn", grouped, picked, preferred_element_type=jnp.float32)
    return kernel.reshape(aux_rows, ntiles, area).astype(jnp.bfloat16)


def shards(three_center, occ_src, occ_block, occ_blocks, virt_block, virt_blocks):
    aux_rows, ntiles, area = three_center.shape
    half = occupied(three_center, occ_src, occ_block, occ_blocks)
    own_blocks = virt_blocks[0]
    listed = virt_block[0]
    all_blocks = lax.all_gather(own_blocks, "pair", axis=0, tiled=True)
    kernel = virtual(half, listed.reshape(ntiles // TPD, TPD, TPD), all_blocks)
    flat_tiles = three_center.reshape(aux_rows, ntiles * area)
    piece = lax.all_gather(kernel, "pair", axis=0, tiled=True)
    flat_piece = piece.reshape(piece.shape[0], ntiles * area)
    partial_value = lax.dot_general(
        flat_tiles, flat_piece, (((1,), (1,)), ((), ())), preferred_element_type=jnp.float32
    )
    return lax.psum_scatter(partial_value, "red", scatter_dimension=1, tiled=True)


def solution(mesh):
    placed = (
        P("pair", "red", None),
        P("red", None),
        P("red", None),
        P("red", None),
        P("red", None, None),
        P("red", "pair", None),
    )
    return jax.shard_map(
        shards, mesh=mesh, in_specs=placed, out_specs=P("pair", "red"), check_vma=False
    )
```

profile of v0, /device:TPU:32, one launch (start us, length us, event | category | flops | bytes accessed | tf_op | source)
XLA Modules:
  0.0 243.4 jit_solution(1345893647742258906)
XLA Ops:
  6.5 0.0 copy-start
  6.5 0.0 copy-start.1
  6.5 0.0 all-gather.3.cloned.1.call-start
  6.5 0.8 copy.21
  7.3 17.9 %all-gather = bf16[1,32,256]{2,0,1:T(2,128)(2,1)S(1)} all-gather(bf16[1,2,256]{2,0,1:T(2,128)(2,1)S(1)} %copy.21), channel_id=2, replica_groups=mesh['pair'=16,'red'=16] {'pair'}, dimensions={1}, use_global_device_ids=true | all-gather | bytes 17408 | tf_op jit(solution)/shard_map/all_gather | solution.py:50
  25.2 0.8 convolution_convert_fusion.2
  26.1 0.1 reshape.42
  26.2 0.0 copy-done
  26.2 1.1 convolution_convert_fusion
  27.3 1.7 reshape.47
  29.0 0.0 copy-done.1
  29.0 1.2 copy.22
  30.2 3.4 %fusion.7 = bf16[144,16,16,16]{0,2,3,1:T(8,128)(2,1)S(1)} fusion(bf16[144,16,16,16]{0,3,2,1:T(8,128)(2,1)S(1)} %bitcast.43, bf16[16,16,16,16,1]{3,2,1,0,4:T(8,128)(2,1)} %reshape.47), kind=kOutput, calls=%fused_computation.7 | convolution fusion | flops 302579712 | bytes 2490368 | tf_op jit(solution)/shard_map/tkml,pkln->ptmn/dot_general | solution.py:27
  33.5 2.2 fusion.4
  35.7 3.7 %copy.26 = bf16[144,16,256]{2,0,1:T(8,128)(2,1)} copy(bf16[144,16,256]{0,2,1:T(8,128)(2,1)} %bitcast.44) | data formatting | bytes 2359296 | tf_op jit(solution)/shard_map/convert_element_type | solution.py:42
  39.4 0.0 all-gather.3.cloned.1.call-update
  39.4 0.0 reduce-scatter.4.cloned.1.call-start
  39.5 103.4 %all-gather.3.cloned.1.call-done = bf16[2304,16,256]{2,0,1:T(8,128)(2,1)} async-done(((bf16[144,16,256]{2,0,1:T(8,128)(2,1)}), bf16[2304,16,256]{2,0,1:T(8,128)(2,1)}) %all-gather.3.cloned.1.call-update) | async-done | bytes 18874384 | tf_op jit(solution)/shard_map/all_gather | solution.py:53
  142.8 9.5 %convolution_bitcast_fusion = f32[144,2304]{1,0:T(8,128)S(1)} fusion(bf16[2304,16,256]{2,0,1:T(8,128)(2,1)} %all-gather.3.cloned.1.call-done, bf16[144,16,256]{0,2,1:T(8,128)(2,1)S(1)} %copy.22), kind=kOutput, calls=%fused_computation.1 | convolution fusion | flops 2717908992 | bytes 21381120 | tf_op jit(solution)/shard_map/dot_general | solution.py:55
  152.3 1.9 copy.33
  154.2 0.0 reduce-scatter.4.cloned.1.call-update
  154.3 80.6 %reduce-scatter.4.cloned.1.call-done = f32[144,144]{1,0:T(8,128)} async-done(((f32[2304,144]{1,0:T(8,128)}), f32[144,144]{1,0:T(8,128)}) %reduce-scatter.4.cloned.1.call-update) | async-done | bytes 82960
  234.9 1.7 copy.34
Async XLA Ops:
  6.5 19.6 %copy-start = (bf16[32,256]{1,0:T(8,128)(2,1)S(1)}, bf16[32,256]{1,0:T(8,128)(2,1)}, u32[]{:S(2)}) copy-start(bf16[32,256]{1,0:T(8,128)(2,1)} %param.9) | copy-start | bytes 49156
  6.5 22.4 %copy-start.1 = (bf16[144,16,256]{2,1,0:T(8,128)(2,1)S(1)}, bf16[144,16,256]{2,1,0:T(8,128)(2,1)}, u32[]{:S(2)}) copy-start(bf16[144,16,256]{2,1,0:T(8,128)(2,1)} %param.6) | copy-start | bytes 3538948
  6.5 136.3 %all-gather.3.cloned.1.call-start = ((), (), s32[]{:S(2)}) async-start(), calls=%async_computation.1 | async-start | bytes 20054016 | tf_op jit(solution)/shard_map/all_gather | solution.py:53
  39.4 195.4 %reduce-scatter.4.cloned.1.call-start = ((), (), s32[]{:S(2)}) async-start(), calls=%async_computation.2 | async-start | bytes 2506752
Sparse Core Ops, SparseCore 0:
  39.6 103.2 all-gather.2
  154.4 80.4 reduce-scatter.3
where the time goes:
time: 244 us; the launch traced here: 243 us
  waiting for transfers between devices  184 us (75%)
  blocking collectives  17.9 us (7%)
  matrix products  17 us (7%)
  between operations  13.4 us (5%)
  local copies, waits for them, and re-layouts  11 us (5%)
    all_gather x1, waiting for transfers between devices, shards(): piece = lax.all_gather(kernel, 'pair', axis=0, tiled=True)  103 us
    unnamed x3, waiting for transfers between devices  80.6 us
    all_gather x1, blocking collectives, shards(): all_blocks = lax.all_gather(own_blocks, 'pair', axis=0, tiled=True)  17.9 us
    dot_general x1, matrix products, shards(): lax.dot_general(flat_tiles, flat_piece, (((1,), (1,)), ((), ())), preferr...  9.48 us
    unnamed x8, local copies, waits for them, and re-layouts  5.55 us
  transfers between devices with their start and end apart: 2, of which 2 were waited for; matrix products, arithmetic and copies ran while one was open for 0% of the time, Pallas kernels for 0%

commit v1 on v0

--- a/solution.py
+++ b/solution.py
@@ -50,7 +50,8 @@
     all_blocks = lax.all_gather(own_blocks, "pair", axis=0, tiled=True)
     kernel = virtual(half, listed.reshape(ntiles // TPD, TPD, TPD), all_blocks)
     flat_tiles = three_center.reshape(aux_rows, ntiles * area)
-    piece = lax.all_gather(kernel, "pair", axis=0, tiled=True)
+    sent = jnp.stack([kernel] * lax.axis_size("pair"))
+    piece = jnp.concatenate(lax.all_to_all(sent, "pair", 0, 0), axis=0)
     flat_piece = piece.reshape(piece.shape[0], ntiles * area)
     partial_value = lax.dot_general(
         flat_tiles, flat_piece, (((1,), (1,)), ((), ())), preferred_element_type=jnp.float32

time: 244 us -> 566 us (2.32)
  waiting for transfers between devices: 184 us -> 488 us
  local copies, waits for them, and re-layouts: 11 us -> 28.4 us
  starting transfers between devices: 0.04 us -> 7.38 us
  matrix products: 17 us -> 9.9 us
    all_to_all x0 -> x1, waiting for transfers between devices: none -> 407 us  [shards(): piece = jnp.concatenate(lax.all_to_all(sent, 'pair', 0, 0), axis=0)]
    all_gather x1 -> x0, waiting for transfers between devices: 103 us -> none  [shards(): piece = lax.all_gather(kernel, 'pair', axis=0, tiled=True)]
    unnamed x8 -> x20, local copies, waits for them, and re-layouts: 5.55 us -> 19.7 us
    all_to_all x0 -> x1, starting transfers between devices: none -> 7.34 us  [shards(): piece = jnp.concatenate(lax.all_to_all(sent, 'pair', 0, 0), axis=0)]
    another operation x1 -> x2, local copies, waits for them, and re-layouts: 0.1 us -> 6.75 us  [the longest x1 6.64 us: shards(): sent = jnp.stack([kernel] * lax.axis_size('pair'))]
    unnamed x3 -> x2, waiting for transfers between devices: 80.6 us -> 81.3 us
where the time goes in v1:
time: 566 us
  waiting for transfers between devices  488 us (86%)
  local copies, waits for them, and re-layouts  28.4 us (5%)
  blocking collectives  17.9 us (3%)
  between operations  13.5 us (2%)
  matrix products  9.9 us (2%)
  starting transfers between devices  7.38 us (1%)
    all_to_all x1, waiting for transfers between devices, shards(): piece = jnp.concatenate(lax.all_to_all(sent, 'pair', 0, 0), axis=0)  407 us
    unnamed x2, waiting for transfers between devices  81.3 us
    unnamed x20, local copies, waits for them, and re-layouts  19.7 us
    all_gather x1, blocking collectives, shards(): all_blocks = lax.all_gather(own_blocks, 'pair', axis=0, tiled=True)  17.9 us
  transfers between devices with their start and end apart: 2, of which 2 were waited for; matrix products, arithmetic and copies ran while one was open for 0% of the time, Pallas kernels for 0%

profile of v1, /device:TPU:32, one launch (start us, length us, event | category | flops | bytes accessed | tf_op | source)
XLA Modules:
  0.0 565.6 jit_solution(9826902022894653531)
XLA Ops:
  6.5 0.0 copy-start
  6.5 0.0 copy-start.4
  6.5 0.0 copy-start.3
  6.5 0.0 copy-start.5
  6.5 0.0 copy-start.6
  6.5 2.7 copy.19
  9.3 0.0 copy-done
  9.3 0.0 copy-done.4
  9.3 0.0 copy-done.3
  9.3 0.4 convolution_convert_fusion
  9.7 0.7 reshape.52
  10.4 0.0 copy-done.5
  10.4 17.9 %all-gather = bf16[1,32,256]{2,0,1:T(2,128)(2,1)S(1)} all-gather(bf16[1,2,256]{2,0,1:T(2,128)(2,1)S(1)} %copy.18), channel_id=2, replica_groups=mesh['pair'=16,'red'=16] {'pair'}, dimensions={1}, use_global_device_ids=true | all-gather | bytes 17408 | tf_op jit(solution)/shard_map/all_gather | solution.py:50
  28.4 0.0 copy-done.6
  28.4 0.2 convolution_convert_fusion.2
  28.6 0.1 reshape.46
  28.7 2.2 fusion.7
  30.8 0.8 fusion.4
  31.7 1.3 copy.23
  33.0 6.6 %stack.2 = bf16[16,144,16,256]{3,2,1,0:T(8,128)(2,1)} broadcast(bf16[144,16,256]{2,1,0:T(8,128)(2,1)S(1)} %copy.23), dimensions={1,2,3} | broadcast | bytes 20054016 | tf_op jit(solution)/shard_map/stack | solution.py:53
  39.6 0.0 copy-start.2
  39.6 7.3 %all-to-all-start = ((bf16[16,144,16,256]{3,2,1,0:T(8,128)(2,1)}), bf16[16,144,16,256]{3,2,1,0:T(8,128)(2,1)}, u32[]{:S(2)}, u32[]{:S(2)}) async-start(bf16[16,144,16,256]{3,2,1,0:T(8,128)(2,1)} %stack.2), calls=%async_computation | async-start | bytes 37748736 | tf_op jit(solution)/shard_map/all_to_all | solution.py:54
  47.0 0.0 reduce-scatter.4.cloned.1.call-start
  47.0 0.0 copy-done.2
  47.0 0.5 copy.33
  47.5 407.2 %all-to-all-done = bf16[16,144,16,256]{3,2,1,0:T(8,128)(2,1)} async-done(((bf16[16,144,16,256]{3,2,1,0:T(8,128)(2,1)}), bf16[16,144,16,256]{3,2,1,0:T(8,128)(2,1)}, u32[]{:S(2)}, u32[]{:S(2)}) %all-to-all-start) | async-done | bytes 18874400 | tf_op jit(solution)/shard_map/all_to_all | solution.py:54
  454.7 12.8 %copy.32 = bf16[288,8,16,256]{3,1,2,0:T(8,128)(2,1)S(1)} copy(bf16[288,8,16,256]{3,2,1,0:T(8,128)(2,1)} %bitcast.21) | data formatting | bytes 37748736
  467.6 6.3 %convolution_bitcast_fusion = f32[144,2304]{1,0:T(8,128)S(1)} fusion(bf16[2304,4096]{1,0:T(8,128)(2,1)S(1)} %bitcast.45, bf16[144,4096]{1,0:T(8,128)(2,1)S(1)} %bitcast.50), kind=kOutput, calls=%fused_computation.1 | convolution fusion | flops 2717908992 | bytes 21381120 | tf_op jit(solution)/shard_map/dot_general | solution.py:56
  473.9 0.0 copy-start.1
  473.9 1.9 copy.29
  475.8 0.0 reduce-scatter.4.cloned.1.call-update
  475.8 81.3 %reduce-scatter.4.cloned.1.call-done = f32[144,144]{1,0:T(8,128)} async-done(((f32[2304,144]{1,0:T(8,128)}), f32[144,144]{1,0:T(8,128)}) %reduce-scatter.4.cloned.1.call-update) | async-done | bytes 82960
  557.1 1.7 copy.30
  558.8 0.0 copy-done.1
  (1 shorter events, 0.0 us)
Async XLA Ops:
  6.5 2.8 copy-start
  6.5 2.8 copy-start.4
  6.5 2.8 copy-start.3
  6.5 3.9 copy-start.5
  6.5 21.8 %copy-start.6 = (s32[1,16,1]{1,2,0:T(1,128)S(1)}, s32[1,16,1]{1,2,0:T(1,128)}, u32[]{:S(2)}) copy-start(s32[1,16,1]{1,2,0:T(1,128)} %param.10) | copy-start | bytes 196
  39.6 7.4 %copy-start.2 = (bf16[144,16,256]{2,1,0:T(8,128)(2,1)S(1)}, bf16[144,16,256]{2,1,0:T(8,128)(2,1)}, u32[]{:S(2)}) copy-start(bf16[144,16,256]{2,1,0:T(8,128)(2,1)} %param.6) | copy-start | bytes 3538948
  39.6 415.1 %all-to-all-start = ((bf16[16,144,16,256]{3,2,1,0:T(8,128)(2,1)}), bf16[16,144,16,256]{3,2,1,0:T(8,128)(2,1)}, u32[]{:S(2)}, u32[]{:S(2)}) async-start(bf16[16,144,16,256]{3,2,1,0:T(8,128)(2,1)} %stack.2), calls=%async_computation | async-start | bytes 37748736 | tf_op jit(solution)/shard_map/all_to_all | solution.py:54
  47.0 510.1 %reduce-scatter.4.cloned.1.call-start = ((), (), s32[]{:S(2)}) async-start(), calls=%async_computation.2 | async-start | bytes 2506752
  473.9 84.9 %copy-start.1 = (bf16[32,256]{1,0:T(8,128)(2,1)S(1)}, bf16[32,256]{1,0:T(8,128)(2,1)}, u32[]{:S(2)}) copy-start(bf16[32,256]{1,0:T(8,128)(2,1)} %param.9) | copy-start | bytes 49156
Sparse Core Ops, SparseCore 0:
  476.0 81.0 reduce-scatter.3
